TPU v7x, 512 devices: a whole 4x8x8 slice. The times are simulated.
512 devices in a mesh: sec: 32 (over z, x), op: 16 (over y, core).
Axes of the slice: x: 4, y: 8, z: 8, core: 2. Of those that a mesh axis runs over, the one named last changes fastest.
Arguments:
- state: float32 [32, 256, 256], P('sec'), may hold values from -6 to 6
- left_ops: float32 [128, 32, 256, 256], P('op', 'sec'), may hold values from -0.03125 to 0.03125
- right_ops: float32 [128, 32, 256, 256], P('op', 'sec'), may hold values from -0.375 to 0.375
- term_shift: int32 [128], P('op'), may hold values from -1 to 1
- sector_rows: int32 [32], P('sec'), may hold values from 128 to 256, as said below
- sector_cols: int32 [32], P('sec'), may hold values from 128 to 256, as said below
Outputs:
- correction: float32 [32, 256, 256], P('sec')
- image: float32 [32, 256, 256], P('sec')
Inputs may be any that keep to these rules, and one draw needn't show every extreme that they name: `sector_rows`: at least one sector has 256 live rows. `sector_cols`: at least one sector has 256 live columns.
All inputs are finite; a program needn't handle non-finite values.
Results may differ from a plain program's by a relative error of at most 0.0003.
Values sent between devices are 32-bit elements; how exact they have to be, the bound alone decides.
A program may use at most 64 MiB of HBM per device.

v0:
```python
import jax
import jax.numpy as jnp
from jax import lax
from jax.sharding import PartitionSpec as P


def padded_2(block, sides, width):
    for axis, dim in sides:
        count = lax.axis_size(axis)
        forward = [(i, i + 1) for i in range(count - 1)]
        backward = [(target, source) for source, target in forward]
        low = lax.ppermute(
            lax.slice_in_dim(block, block.shape[dim] - width, None, axis=dim), axis, forward
        )
        high = lax.ppermute(lax.slice_in_dim(block, 0, width, axis=dim), axis, backward)
        block = jnp.concatenate([low, block, high], axis=dim)
    return block


def live_mask(sector_rows, sector_cols, block):
    place = jnp.arange(block, dtype=jnp.int32)
    rows_ok = place[None, :, None] < sector_rows[:, None, None]
    cols_ok = place[None, None, :] < sector_cols[:, None, None]
    return (rows_ok & cols_ok).astype(jnp.float32)


def apply_terms(field, left_ops, right_ops, term_shift):
    count = field.shape[0]
    padded = padded_2(field, (("sec", 0),), 1)
    total = jnp.zeros(field.shape, jnp.float32)
    for term in range(left_ops.shape[0]):
        start = 1 - term_shift[term]
        source = lax.dynamic_slice_in_dim(padded, start, count, 0)
        inner = jnp.einsum("tij,tjl->til", left_ops[term], source, precision=lax.Precision.HIGHEST)
        total = total + jnp.einsum(
            "til,tml->tim", inner, right_ops[term], precision=lax.Precision.HIGHEST
        )
    return total


def local(state, left_ops, right_ops, term_shift, sector_rows, sector_cols):
    block = state.shape[1]
    mask = live_mask(sector_rows, sector_cols, block)
    field = state * mask
    cells = state.shape[0] * lax.axis_size("sec") * block * block

    def whole_product(vector):
        partial_sum = apply_terms(vector, left_ops, right_ops, term_shift)
        return lax.psum(partial_sum, "op") * mask

    first = whole_product(field)
    cross, square = lax.psum((jnp.sum(field * first), jnp.sum(field * field)), "sec")
    theta = cross / square
    resid = first - theta * field
    energy = lax.psum(jnp.sum(resid * resid), "sec")
    correction = resid * lax.rsqrt(energy / cells + 1e-06)
    image = whole_product(correction)
    return (correction, image)


def solution(mesh):
    in_specs = (
        P("sec", None, None),
        P("op", "sec", None, None),
        P("op", "sec", None, None),
        P("op"),
        P("sec"),
        P("sec"),
    )
    out_specs = (P("sec", None, None), P("sec", None, None))
    return jax.shard_map(local, mesh=mesh, in_specs=in_specs, out_specs=out_specs, check_vma=False)
```

profile of v0, /device:TPU:1, one launch (start us, length us, event | category | flops | bytes accessed | tf_op | source)
XLA Modules:
  0.0 459.9 jit_solution(17721254046100964716)
XLA Ops:
  8.5 1.1 and_select_fusion.2
  9.6 4.0 collective-permute-start
  13.5 1.3 collective-permute-start.1
  14.8 1.6 fusion.132
  26.8 1.7 fusion.65
  28.5 1.6 fusion.57
  30.1 1.6 fusion.51
  31.7 1.7 fusion.45
  34.0 0.6 fusion.33
  34.6 0.6 fusion.27
  35.2 0.6 fusion.21
  40.1 1.3 fusion.1
  41.5 120.8 %all-reduce.4.cloned.1.call-done = f32[1,256,256]{2,1,0:T(8,128)} async-done(((f32[1,256,256]{2,1,0:T(8,128)}), f32[1,256,256]{2,1,0:T(8,128)}) %all-reduce.4.cloned.1.call-update) | async-done | bytes 262160 | tf_op jit(solution)/shard_map/psum | solution.py:49
  162.3 1.7 multiply_reduce_fusion.1
  164.0 62.1 %all-reduce = (f32[]{:T(128)}, f32[]{:T(128)}) all-reduce(f32[]{:T(128)} %get-tuple-element.3, f32[]{:T(128)} %get-tuple-element.2), channel_id=1, replica_groups=mesh['sec'=32,'op'=16] {'sec'}, use_global_device_ids=true, to_apply=%region_2.0 | all-reduce | flops 2 | bytes 16 | tf_op jit(solution)/shard_map/psum | solution.py:52
  227.5 1.7 multiply_reduce_fusion
  229.2 56.7 %psum.38 = f32[]{:T(128)} all-reduce(f32[]{:T(128)} %multiply_reduce_fusion), channel_id=1, replica_groups=mesh['sec'=32,'op'=16] {'sec'}, use_global_device_ids=true, to_apply=%region_6.0 | all-reduce | flops 1 | bytes 8 | tf_op jit(solution)/shard_map/psum | solution.py:55
  286.6 1.2 broadcast_multiply_fusion
  287.8 3.0 collective-permute-start.2
  290.8 1.5 collective-permute-start.3
  292.3 1.8 collective-permute-done.2
  294.1 3.8 collective-permute-done.3
  298.6 0.6 fusion.14
  299.2 0.6 fusion.12
  299.9 0.6 fusion.10
  300.5 0.6 fusion.8
  301.1 0.6 fusion.6
  301.7 0.6 fusion.4
  302.3 0.6 fusion.2
  307.2 1.3 fusion
  308.5 142.8 %all-reduce.6.cloned.1.call-done = f32[1,256,256]{2,1,0:T(8,128)} async-done(((f32[1,256,256]{2,1,0:T(8,128)}), f32[1,256,256]{2,1,0:T(8,128)}) %all-reduce.6.cloned.1.call-update) | async-done | bytes 262160 | tf_op jit(solution)/shard_map/psum | solution.py:49
  451.3 1.8 and_select_fusion
  (35 shorter events, 9.9 us)
Async XLA Ops:
  7.2 155.1 %all-reduce.4.cloned.1.call-start = ((), (), s32[]{:S(2)}) async-start(), calls=%async_computation | async-start | bytes 524288 | tf_op jit(solution)/shard_map/psum | solution.py:49
  9.6 17.2 %collective-permute-start = (f32[1,256,256]{2,1,0:T(8,128)S(1)}, f32[1,256,256]{2,1,0:T(8,128)S(1)}, u32[]{:S(2)}, u32[]{:S(2)}) collective-permute-start(f32[1,256,256]{2,1,0:T(8,128)S(1)} %and_select_fusion.2), channel_id=1, source_target_pairs={{0,16},{16,32},{32,48},{48,64},{64,80},{80,96},{96,112},{112,128},... | collective-permute-start | bytes 786440 | tf_op jit(solution)/shard_map/ppermute | solution.py:12
  13.5 13.2 %collective-permute-start.1 = (f32[1,256,256]{2,1,0:T(8,128)S(1)}, f32[1,256,256]{2,1,0:T(8,128)S(1)}, u32[]{:S(2)}, u32[]{:S(2)}) collective-permute-start(f32[1,256,256]{2,1,0:T(8,128)S(1)} %and_select_fusion.2), channel_id=1, source_target_pairs={{16,0},{32,16},{48,32},{64,48},{80,64},{96,80},{112,96},{128,112},... | collective-permute-start | bytes 786440 | tf_op jit(solution)/shard_map/ppermute | solution.py:15
  26.7 6.7 %copy-start.1 = (f32[8,1,256,256]{3,2,1,0:T(8,128)S(1)}, f32[8,1,256,256]{3,2,1,0:T(8,128)}, u32[]{:S(2)}) copy-start(f32[8,1,256,256]{3,2,1,0:T(8,128)} %param.7) | copy-start | bytes 6291460
  31.7 4.2 copy-start
  38.3 124.0 %copy-start.3 = (f32[1,256,256]{2,1,0:T(8,128)S(1)}, f32[1,256,256]{2,1,0:T(8,128)}, u32[]{:S(2)}) copy-start(f32[1,256,256]{2,1,0:T(8,128)} %param.6) | copy-start | bytes 786436
  41.5 409.9 %all-reduce.6.cloned.1.call-start = ((), (), s32[]{:S(2)}) async-start(), calls=%async_computation.1 | async-start | bytes 524288 | tf_op jit(solution)/shard_map/psum | solution.py:49
  286.6 11.5 %copy-start.2 = (f32[8,1,256,256]{3,2,1,0:T(8,128)S(1)}, f32[8,1,256,256]{3,2,1,0:T(8,128)}, u32[]{:S(2)}) copy-start(f32[8,1,256,256]{3,2,1,0:T(8,128)} %param.7) | copy-start | bytes 6291460
  287.8 12.7 %copy-start.4 = (f32[1,256,256]{2,1,0:T(8,128)}, f32[1,256,256]{2,1,0:T(8,128)S(1)}, u32[]{:S(2)}) copy-start(f32[1,256,256]{2,1,0:T(8,128)S(1)} %broadcast_multiply_fusion) | copy-start | bytes 786436
  287.8 6.3 %collective-permute-start.2 = (f32[1,256,256]{2,1,0:T(8,128)S(1)}, f32[1,256,256]{2,1,0:T(8,128)S(1)}, u32[]{:S(2)}, u32[]{:S(2)}) collective-permute-start(f32[1,256,256]{2,1,0:T(8,128)S(1)} %broadcast_multiply_fusion), channel_id=1, source_target_pairs={{0,16},{16,32},{32,48},{48,64},{64,80},{80,96},{96,112},{112,128},... | collective-permute-start | bytes 786440 | tf_op jit(solution)/shard_map/ppermute | solution.py:12
  290.8 7.1 %collective-permute-start.3 = (f32[1,256,256]{2,1,0:T(8,128)S(1)}, f32[1,256,256]{2,1,0:T(8,128)S(1)}, u32[]{:S(2)}, u32[]{:S(2)}) collective-permute-start(f32[1,256,256]{2,1,0:T(8,128)S(1)} %broadcast_multiply_fusion), channel_id=1, source_target_pairs={{16,0},{32,16},{48,32},{64,48},{80,64},{96,80},{112,96},{128,112},... | collective-permute-start | bytes 786440 | tf_op jit(solution)/shard_map/ppermute | solution.py:15
Sparse Core Ops, SparseCore 0:
  41.6 120.6 all-reduce.3
  308.6 142.6 all-reduce.5
where the time goes:
time: 461 us; the launch traced here: 460 us
  waiting for transfers between devices  269 us (58%)
  blocking collectives  119 us (26%)
  between operations  28 us (6%)
  matrix products  24.8 us (5%)
  starting transfers between devices  9.82 us (2%)
  other arithmetic  7.55 us (2%)
    psum x2, waiting for transfers between devices, whole_product(): return lax.psum(partial_sum, 'op') * mask  264 us
    psum x1, blocking collectives, local(): lax.psum((jnp.sum(field * first), jnp.sum(field * field)), 'sec')  62.1 us
    psum x1, blocking collectives, local(): energy = lax.psum(jnp.sum(resid * resid), 'sec')  56.7 us
    dot_general x16, matrix products, apply_terms(): jnp.einsum('tij,tjl->til', left_ops[term], source, precision=lax.Precisio...  13.8 us
    dot_general x16, matrix products, apply_terms(): jnp.einsum('til,tml->tim', inner, right_ops[term], precision=lax.Precisio...  11 us
  transfers between devices with their start and end apart: 6, of which 4 were waited for; matrix products, arithmetic and copies ran while one was open for 0% of the time, Pallas kernels for 0%

commit v1 on v0

v1 whole, which is shorter than its diff:
```python
import functools

import jax
import jax.numpy as jnp
from jax import lax
from jax.experimental import pallas as pl
from jax.experimental.pallas import tpu as pltpu
from jax.sharding import PartitionSpec as P

MESH = pl.DeviceIdType.MESH
SEC_X = 4
LANES = 128
NN = (((1,), (0,)), ((), ()))
NT = (((1,), (1,)), ((), ()))


def split(value):
    high = value.astype(jnp.bfloat16)
    return high, (value - high.astype(jnp.float32)).astype(jnp.bfloat16)


def dot(a, b, dims):
    return lax.dot_general(a, b, dims, preferred_element_type=jnp.float32)


def dot3(a_high, a_low, b_high, b_low, dims):
    return dot(a_high, b_high, dims) + (dot(a_low, b_high, dims) + dot(a_high, b_low, dims))


def kernel(
    sizes,
    state, left, right, shift, rows, cols,
    corr, image,
    state_v, left_f, right_f, shift_s, rows_s, cols_s,
    left_c, right_c, vec_c,
    field, near1, near2, part1, part2, sib1, sib2, sum1, sum2, box1, box2,
    full, full_i, scal_x, scal_z,
    local_sem, send_sem, recv_sem,
):
    n_sec, n_op, terms, block = sizes
    n_x = min(SEC_X, n_sec)
    n_z = n_sec // n_x
    n_y = n_op // 2
    piece = block // n_y
    s, o = lax.axis_index("sec"), lax.axis_index("op")
    y, c = o // 2, o % 2
    x, z = s % n_x, s // n_x
    mate = (s, y * 2 + (1 - c))
    after, before = ((s + 1) % n_sec, o), ((s + n_sec - 1) % n_sec, o)
    along_y = [(s, ((y + d) % n_y) * 2 + c) for d in range(1, n_y)]
    along_x = [(z * n_x + (x + d) % n_x, o) for d in range(1, n_x)]
    along_z = [(((z + d) % n_z) * n_x + x, o) for d in range(1, n_z)]

    count = [0]
    sent = []

    def remote(src, dst, device):
        i = count[0]
        count[0] += 1
        copy = pltpu.make_async_remote_copy(
            src_ref=src, dst_ref=dst, send_sem=send_sem.at[i], recv_sem=recv_sem.at[i],
            device_id=device, device_id_type=MESH,
        )
        copy.start()
        sent.append(copy)
        return copy

    partners = [mate, after, before] + along_y + along_x + along_z
    barrier = pltpu.get_barrier_semaphore()
    for device in partners:
        pl.semaphore_signal(barrier, inc=1, device_id=device, device_id_type=MESH)

    local = [
        pltpu.make_async_copy(src, dst, local_sem.at[i])
        for i, (src, dst) in enumerate(
            [(state.at[0], state_v), (rows, rows_s), (cols, cols_s), (shift, shift_s),
             (left.at[:, 0], left_f), (right.at[:, 0], right_f)]
        )
    ]
    for copy in local:
        copy.start()
    for copy in local[:3]:
        copy.wait()
    n_rows, n_cols = rows_s[0], cols_s[0]

    def masked(value, row0, col0):
        at_row = lax.broadcasted_iota(jnp.int32, value.shape, 0) + row0
        at_col = lax.broadcasted_iota(jnp.int32, value.shape, 1) + col0
        return value * ((at_row < n_rows) & (at_col < n_cols)).astype(jnp.float32)

    for h in range(2):
        field[h] = masked(state_v[:, h * LANES:(h + 1) * LANES], 0, h * LANES)
    pl.semaphore_wait(barrier, len(partners))

    def send_half(src, near):
        return [remote(src.at[c], near.at[0, c], after), remote(src.at[c], near.at[1, c], before)]

    def pass_on(copies, near):
        on = []
        for side in range(2):
            copies[side].wait_recv()
            on.append(remote(near.at[side, c], near.at[side, c], mate))
        return on

    def to_bf16(src, slot, keep=None):
        for h in range(2):
            value = src[h]
            if keep is not None:
                value = jnp.where(keep, value, 0.0)
            high, low = split(value)
            vec_c[slot, 0:block, h * LANES:(h + 1) * LANES] = high
            vec_c[slot, block:2 * block, h * LANES:(h + 1) * LANES] = low

    def product(part):
        total = None
        for k in range(terms):
            at = 1 - shift_s[k]
            inner = dot3(
                left_c[0, k], left_c[1, k], vec_c[at, 0:block], vec_c[at, block:2 * block], NN
            )
            high, low = split(inner)
            term = dot3(high, low, right_c[0, k], right_c[1, k], NT)
            total = term if total is None else total + term
        for h in range(2):
            part[h] = total[:, h * LANES:(h + 1) * LANES]

    mine = pl.ds(pl.multiple_of(y * piece, piece), piece)

    def scatter_sum(part, sib, summed, box, while_waiting=None):
        swap = remote(part.at[1 - c], sib, mate)
        if while_waiting is not None:
            while_waiting()
        swap.wait_recv()
        summed[...] = part[c] + sib[...]
        copies = []
        for d in range(1, n_y):
            to = (y + d) % n_y
            copies.append(
                remote(
                    summed.at[pl.ds(pl.multiple_of(to * piece, piece), piece)],
                    box.at[d], along_y[d - 1],
                )
            )
        total = summed[mine]
        for d in range(1, n_y):
            copies[d - 1].wait_recv()
            total = total + box[d]
        return masked(total, y * piece, c * LANES)

    def gather(whole):
        copies = [
            remote(whole.at[c, mine], whole.at[c, mine], along_y[d - 1]) for d in range(1, n_y)
        ]
        for copy in copies:
            copy.wait_recv()

    copies = send_half(field, near1)
    to_bf16(field, 1)
    for copy in local[3:]:
        copy.wait()
    for k in range(terms):
        left_c[0, k], left_c[1, k] = split(left_f[k])
        right_c[0, k], right_c[1, k] = split(right_f[k])
    for copy in pass_on(copies, near1):
        copy.wait_recv()
    to_bf16(near1.at[0], 0, s > 0)
    to_bf16(near1.at[1], 2, s < n_sec - 1)
    product(part1)
    full[c, mine] = scatter_sum(part1, sib1, sum1, box1)
    gather(full)

    own_half = remote(full.at[c], full.at[c], mate)
    copies = send_half(full, near2)
    own_half.wait_recv()
    to_bf16(full, 1)

    def total_of(terms_of):
        value = terms_of(0) + terms_of(1)
        return jnp.sum(jnp.sum(value, axis=0, keepdims=True), axis=1, keepdims=True)

    square = total_of(lambda h: field[h] * field[h])
    cross = total_of(lambda h: field[h] * full[h])
    own_theta = jnp.where(square > 0, cross / square, 0.0)
    rest = total_of(lambda h: (full[h] - own_theta * field[h]) * (full[h] - own_theta * field[h]))
    at = lax.broadcasted_iota(jnp.int32, (8, LANES), 0)
    scal_x[x] = jnp.where(at == 0, square, jnp.where(at == 1, cross, rest))
    x_copies = [remote(scal_x.at[x], scal_x.at[x], device) for device in along_x]

    for copy in pass_on(copies, near2):
        copy.wait_recv()
    to_bf16(near2.at[0], 0, s > 0)
    to_bf16(near2.at[1], 2, s < n_sec - 1)
    product(part2)
    z_copies = []

    def pass_scalars():
        for copy in x_copies:
            copy.wait_recv()
        scal_z[z] = scal_x[...]
        z_copies.extend(remote(scal_z.at[z], scal_z.at[z], device) for device in along_z)

    second = scatter_sum(part2, sib2, sum2, box2, pass_scalars)
    for copy in z_copies:
        copy.wait_recv()

    def all_of(i):
        return jnp.concatenate([scal_z[a, b, i:i + 1, :] for a in range(n_z) for b in range(n_x)], axis=0)

    squares, crosses, rests = all_of(0), all_of(1), all_of(2)
    thetas = jnp.where(squares > 0, crosses / squares, 0.0)
    theta = jnp.sum(crosses, axis=0, keepdims=True) / jnp.sum(squares, axis=0, keepdims=True)
    gap = (thetas - theta) * jnp.sqrt(squares)
    energy = jnp.sum(rests + gap * gap, axis=0, keepdims=True)
    scale = lax.rsqrt(energy / (n_sec * block * block) + 1e-06)

    full_i[c, mine] = scale * (second - theta * full[c, mine])
    gather(full_i)
    own_half = remote(full_i.at[c], full_i.at[c], mate)
    for h in range(2):
        corr[:, h * LANES:(h + 1) * LANES] = (full[h] - theta * field[h]) * scale
    own_half.wait_recv()
    for h in range(2):
        image[:, h * LANES:(h + 1) * LANES] = full_i[h]
    for copy in sent:
        copy.wait_send()


def local(n_sec, n_op, state, left, right, shift, rows, cols):
    terms, block = left.shape[0], state.shape[1]
    n_x = min(SEC_X, n_sec)
    n_y = n_op // 2
    piece = block // n_y
    f32, bf16 = jnp.float32, jnp.bfloat16
    n_copies = 64
    half = (block, LANES)
    corr, image = pl.pallas_call(
        functools.partial(kernel, (n_sec, n_op, terms, block)),
        out_shape=[jax.ShapeDtypeStruct((block, block), f32)] * 2,
        in_specs=[pl.BlockSpec(memory_space=pl.ANY)] * 6,
        out_specs=[pl.BlockSpec(memory_space=pltpu.VMEM)] * 2,
        scratch_shapes=[
            pltpu.VMEM((block, block), f32),
            pltpu.VMEM((terms, block, block), f32),
            pltpu.VMEM((terms, block, block), f32),
            pltpu.SMEM((terms,), jnp.int32),
            pltpu.SMEM((1,), jnp.int32),
            pltpu.SMEM((1,), jnp.int32),
            pltpu.VMEM((2, terms, block, block), bf16),
            pltpu.VMEM((2, terms, block, block), bf16),
            pltpu.VMEM((3, 2 * block, block), bf16),
            pltpu.VMEM((2,) + half, f32),
            pltpu.VMEM((2, 2) + half, f32),
            pltpu.VMEM((2, 2) + half, f32),
            pltpu.VMEM((2,) + half, f32),
            pltpu.VMEM((2,) + half, f32),
            pltpu.VMEM(half, f32),
            pltpu.VMEM(half, f32),
            pltpu.VMEM(half, f32),
            pltpu.VMEM(half, f32),
            pltpu.VMEM((n_y, piece, LANES), f32),
            pltpu.VMEM((n_y, piece, LANES), f32),
            pltpu.VMEM((2,) + half, f32),
            pltpu.VMEM((2,) + half, f32),
            pltpu.VMEM((n_x, 8, LANES), f32),
            pltpu.VMEM((n_sec // n_x, n_x, 8, LANES), f32),
            pltpu.SemaphoreType.DMA((6,)),
            pltpu.SemaphoreType.DMA((n_copies,)),
            pltpu.SemaphoreType.DMA((n_copies,)),
        ],
        compiler_params=pltpu.CompilerParams(
            collective_id=0, has_side_effects=True, vmem_limit_bytes=40 << 20
        ),
        name="davidson",
    )(state, left, right, shift, rows, cols)
    return corr[None], image[None]


def solution(mesh):
    in_specs = (
        P("sec", None, None),
        P("op", "sec", None, None),
        P("op", "sec", None, None),
        P("op"),
        P("sec"),
        P("sec"),
    )
    out_specs = (P("sec", None, None), P("sec", None, None))
    return jax.shard_map(
        functools.partial(local, mesh.shape["sec"], mesh.shape["op"]),
        mesh=mesh, in_specs=in_specs, out_specs=out_specs, check_vma=False,
    )
```

time: 461 us -> 68.6 us (0.15)
  waiting for transfers between devices: 269 us -> 0 us
  blocking collectives: 119 us -> 0 us
  Pallas kernels: 0 us -> 60.2 us
  between operations: 28 us -> 1.94 us
  matrix products: 24.8 us -> 0 us
  starting transfers between devices: 9.82 us -> 0 us
  other arithmetic: 7.55 us -> 0 us
    psum x2 -> x0, waiting for transfers between devices: 264 us -> none  [whole_product(): return lax.psum(partial_sum, 'op') * mask]
    psum x2 -> x0, blocking collectives: 119 us -> none  [the longest x1 62.1 us: local(): lax.psum((jnp.sum(field * first), jnp.sum(field * field)), 'sec')]
    pallas_call x0 -> x1, Pallas kernels: none -> 60.2 us  [local(): pl.pallas_call(functools.partial(kernel, (n_sec, n_op, terms, block)), ou...]
    dot_general x32 -> x0, matrix products: 24.8 us -> none  [the longest x16 13.8 us: apply_terms(): jnp.einsum('tij,tjl->til', left_ops[term], source, precision=lax.Precisio...]
    ppermute x4 -> x0, starting transfers between devices: 9.74 us -> none  [the longest x2 6.98 us: padded_2(): lax.ppermute(lax.slice_in_dim(block, block.shape[dim] - width, None, axis...]
    unnamed x10, local copies, waits for them, and re-layouts: 0.03 us -> 6.19 us
    ppermute x4 -> x0, waiting for transfers between devices: 5.64 us -> none  [the longest x2 3.84 us: padded_2(): lax.ppermute(lax.slice_in_dim(block, 0, width, axis=dim), axis, backward)]
  transfers between devices with their start and end apart: 6 -> 0, of which waited for: 4 -> 0; matrix products, arithmetic and copies ran while one was open for 0% -> 0% of each run, Pallas kernels for 0% -> 0%
where the time goes in v1:
time: 68.6 us; the launch traced here: 68.3 us
  Pallas kernels  60.2 us (88%)
  local copies, waits for them, and re-layouts  6.19 us (9%)
  between operations  1.94 us (3%)
    pallas_call x1, Pallas kernels, local(): pl.pallas_call(functools.partial(kernel, (n_sec, n_op, terms, block)), ou...  60.2 us
    unnamed x10, local copies, waits for them, and re-layouts  6.19 us

profile of v1, /device:TPU:1, one launch (start us, length us, event | category | flops | bytes accessed | tf_op | source)
XLA Modules:
  0.0 68.3 jit_solution(14538252753572824331)
XLA Ops:
  1.9 0.0 copy-start
  1.9 1.6 %copy-done = f32[8,1,256,256]{3,2,1,0:T(8,128)S(1)} copy-done((f32[8,1,256,256]{3,2,1,0:T(8,128)S(1)}, f32[8,1,256,256]{3,2,1,0:T(8,128)}, u32[]{:S(2)}) %copy-start) | copy-done | bytes 2097176
  3.5 0.0 copy-start.1
  3.5 1.6 %copy-done.1 = f32[8,1,256,256]{3,2,1,0:T(8,128)S(1)} copy-done((f32[8,1,256,256]{3,2,1,0:T(8,128)S(1)}, f32[8,1,256,256]{3,2,1,0:T(8,128)}, u32[]{:S(2)}) %copy-start.1) | copy-done | bytes 2097176
  5.1 0.0 copy-start.2
  5.1 0.9 %copy-done.2 = f32[1,256,256]{2,1,0:T(8,128)S(1)} copy-done((f32[1,256,256]{2,1,0:T(8,128)S(1)}, f32[1,256,256]{2,1,0:T(8,128)}, u32[]{:S(2)}) %copy-start.2) | copy-done | bytes 262168
  6.1 0.0 copy-start.3
  6.1 0.7 copy-done.3
  6.7 60.2 %davidson.1 = (f32[256,256]{1,0:T(8,128)S(1)}, f32[256,256]{1,0:T(8,128)S(1)}) custom-call(f32[1,256,256]{2,1,0:T(8,128)S(1)} %copy-done.2, f32[8,1,256,256]{3,2,1,0:T(8,128)S(1)} %copy-done, f32[8,1,256,256]{3,2,1,0:T(8,128)S(1)} %copy-done.1, s32[8]{0:T(128)S(1)} %copy-done.3, s32[1]{0:T(128)S(6)} %copy.10.rows, s32[1]{0:T(128)S(6)} %copy.11.cols), custom_call_target="tpu_custom_call" | custom-call | tf_op jit(solution)/shard_map/davidson/pallas_call | solution.py:236
  66.9 0.7 %copy.12 = f32[1,256,256]{2,1,0:T(8,128)} copy(f32[1,256,256]{2,1,0:T(8,128)S(1)} %bitcast.3) | data formatting | bytes 524288
  67.6 0.7 %copy.13 = f32[1,256,256]{2,1,0:T(8,128)} copy(f32[1,256,256]{2,1,0:T(8,128)S(1)} %bitcast.2) | data formatting | bytes 524288
Async XLA Ops:
  1.9 1.6 %copy-start = (f32[8,1,256,256]{3,2,1,0:T(8,128)S(1)}, f32[8,1,256,256]{3,2,1,0:T(8,128)}, u32[]{:S(2)}) copy-start(f32[8,1,256,256]{3,2,1,0:T(8,128)} %left.1) | copy-start | bytes 6291460
  3.5 1.6 %copy-start.1 = (f32[8,1,256,256]{3,2,1,0:T(8,128)S(1)}, f32[8,1,256,256]{3,2,1,0:T(8,128)}, u32[]{:S(2)}) copy-start(f32[8,1,256,256]{3,2,1,0:T(8,128)} %right.1) | copy-start | bytes 6291460
  5.1 0.9 %copy-start.2 = (f32[1,256,256]{2,1,0:T(8,128)S(1)}, f32[1,256,256]{2,1,0:T(8,128)}, u32[]{:S(2)}) copy-start(f32[1,256,256]{2,1,0:T(8,128)} %state.1) | copy-start | bytes 786436
  6.1 0.7 copy-start.3

commit v2 on v1

v2 whole, which is shorter than its diff:
```python
import functools

import jax
import jax.numpy as jnp
from jax import lax
from jax.experimental import pallas as pl
from jax.experimental.pallas import tpu as pltpu
from jax.sharding import PartitionSpec as P

MESH = pl.DeviceIdType.MESH
SEC_X = 4
LANES = 128
NEAR_TO_FAR = ((0, 1, 7), (2, 6), (3, 5, 4))
FAR_FIRST = (4, 3, 5, 2, 6, 1, 7)
NN = (((1,), (0,)), ((), ()))
NT = (((1,), (1,)), ((), ()))


def split(value):
    high = value.astype(jnp.bfloat16)
    return high, (value - high.astype(jnp.float32)).astype(jnp.bfloat16)


def dot(a, b, dims):
    return lax.dot_general(a, b, dims, preferred_element_type=jnp.float32)


def dot3(a_high, a_low, b_high, b_low, dims):
    return dot(a_high, b_high, dims) + (dot(a_low, b_high, dims) + dot(a_high, b_low, dims))


def kernel(
    sizes,
    state, left, right, shift, rows, cols,
    corr, image,
    state_v, left_f, right_f, shift_s, rows_s, cols_s,
    left_c, right_c, vec_c,
    field, near1, near2, part1, part2, sib1, sib2, sum1, sum2, box1, box2,
    full, last, counts, near_counts, scal_x, scal_z,
    local_sem, send_sem, recv_sem,
):
    n_sec, n_op, terms, block = sizes
    n_x = min(SEC_X, n_sec)
    n_z = n_sec // n_x
    n_y = n_op // 2
    half = block // 2
    piece = half // n_y
    order = [d for group in NEAR_TO_FAR for d in group]
    at_slot = {d: i for i, d in enumerate(order)}
    s, o = lax.axis_index("sec"), lax.axis_index("op")
    y, c = o // 2, o % 2
    x, z = s % n_x, s // n_x
    mate = (s, y * 2 + (1 - c))
    after, before = ((s + 1) % n_sec, o), ((s + n_sec - 1) % n_sec, o)
    along_y = {d: (s, ((y + d) % n_y) * 2 + c) for d in FAR_FIRST}
    along_x = [(z * n_x + (x + d) % n_x, o) for d in range(1, n_x)]
    along_z = [(((z + d) % n_z) * n_x + x, o) for d in range(1, n_z)]

    count = [0]
    sent = []

    def remote(src, dst, device):
        i = count[0]
        count[0] += 1
        copy = pltpu.make_async_remote_copy(
            src_ref=src, dst_ref=dst, send_sem=send_sem.at[i], recv_sem=recv_sem.at[i],
            device_id=device, device_id_type=MESH,
        )
        copy.start()
        sent.append(copy)
        return copy

    def tile_rows(index, size):
        return pl.ds(pl.multiple_of(index * size, size), size)

    partners = [mate, after, before, *along_y.values(), *along_x, *along_z]
    barrier = pltpu.get_barrier_semaphore()
    for device in partners:
        pl.semaphore_signal(barrier, inc=1, device_id=device, device_id_type=MESH)

    def load(i, src, dst):
        copy = pltpu.make_async_copy(src, dst, local_sem.at[i])
        copy.start()
        return copy

    small = [load(0, rows, rows_s), load(1, cols, cols_s), load(2, shift, shift_s)]
    pl.semaphore_wait(barrier, len(partners))

    to_after = remote(state.at[0, tile_rows(c, half)], near1.at[0, c], after)
    to_before = remote(state.at[0, tile_rows(c, half)], near1.at[1, c], before)
    own_state = load(3, state.at[0], state_v)
    operators = [load(4, left.at[:, 0], left_f), load(5, right.at[:, 0], right_f)]
    for copy in small:
        copy.wait()
    n_rows, n_cols = rows_s[0], cols_s[0]
    at = lax.broadcasted_iota(jnp.int32, counts.shape, 0)
    counts[...] = jnp.where(at == 0, n_rows, n_cols)
    count_copies = [
        remote(counts, near_counts.at[0], after), remote(counts, near_counts.at[1], before)
    ]

    def masked(value, row0, some_rows, some_cols):
        at_row = lax.broadcasted_iota(jnp.int32, value.shape, 0) + row0
        at_col = lax.broadcasted_iota(jnp.int32, value.shape, 1)
        return value * ((at_row < some_rows) & (at_col < some_cols)).astype(jnp.float32)

    def hold(slot, where, value):
        high, low = split(value)
        vec_c[slot, 0, where] = high
        vec_c[slot, 1, where] = low

    def product(part):
        total = None
        for k in range(terms):
            source = 1 - shift_s[k]
            inner = dot3(left_c[0, k], left_c[1, k], vec_c[source, 0], vec_c[source, 1], NN)
            high, low = split(inner)
            term = dot3(high, low, right_c[0, k], right_c[1, k], NT)
            total = term if total is None else total + term
        part[0] = total[:half]
        part[1] = total[half:]

    def scatter_sum(part, sib, summed, box):
        swap = remote(part.at[1 - c], sib, mate)
        swap.wait_recv()
        summed[...] = part[c] + sib[...]
        copies = {}
        for d in FAR_FIRST:
            to = (y + d) % n_y
            copies[d] = remote(summed.at[tile_rows(to, piece)], box.at[d], along_y[d])
        total = summed[tile_rows(y, piece)]
        for d in order[1:]:
            copies[d].wait_recv()
            total = total + box[d]
        return masked(total, c * half + y * piece, n_rows, n_cols)

    def exist(side):
        return s > 0 if side == 0 else s < n_sec - 1

    own_state.wait()
    field[...] = masked(state_v[...], 0, n_rows, n_cols)
    hold(1, slice(None), field[...])
    for copy in operators:
        copy.wait()
    for k in range(terms):
        left_c[0, k], left_c[1, k] = split(left_f[k])
        right_c[0, k], right_c[1, k] = split(right_f[k])
    passed = []
    for side, copy in enumerate((to_after, to_before)):
        copy.wait_recv()
        passed.append(remote(near1.at[side, c], near1.at[side, c], mate))

    def hold_near(side, part_of):
        some_rows = jnp.where(exist(side), near_counts[side, 0:1, :], 0)
        row0 = part_of * half
        value = masked(near1[side, part_of], row0, some_rows, near_counts[side, 1:2, :])
        hold(2 * side, tile_rows(part_of, half), value)

    for side in range(2):
        count_copies[side].wait_recv()
        hold_near(side, c)
    for side in range(2):
        passed[side].wait_recv()
        hold_near(side, 1 - c)
    product(part1)
    full[c, 0] = scatter_sum(part1, sib1, sum1, box1)

    copies = {d: remote(full.at[c, 0], full.at[c, at_slot[n_y - d]], along_y[d]) for d in FAR_FIRST}
    groups, first = [], 0
    for group in NEAR_TO_FAR:
        groups.append((group, pl.ds(first, len(group))))
        first += len(group)
    onward = []
    for group, slots in groups:
        for d in group:
            if d:
                copies[n_y - d].wait_recv()
        here = full.at[c, slots]
        onward.append((
            remote(here, near2.at[0, c, slots], after),
            remote(here, near2.at[1, c, slots], before),
            remote(here, full.at[c, slots], mate),
        ))

    def rows_of(part_of, d):
        return pl.ds(pl.multiple_of(part_of * half + (y + d) % n_y * piece, piece), piece)

    def hold_full(part_of, group):
        for d in group:
            hold(1, rows_of(part_of, d), full[part_of, at_slot[d]])

    for group, slots in groups:
        hold_full(c, group)
    for (group, slots), copy in zip(groups, onward):
        copy[2].wait_recv()
        hold_full(1 - c, group)

    def total_of(term):
        value = None
        for part_of in range(2):
            for d in order:
                add = term(field[rows_of(part_of, d)], full[part_of, at_slot[d]])
                value = add if value is None else value + add
        return jnp.sum(jnp.sum(value, axis=0, keepdims=True), axis=1, keepdims=True)

    square = total_of(lambda f, g: f * f)
    cross = total_of(lambda f, g: f * g)
    own_theta = jnp.where(square > 0, cross / square, 0.0)
    rest = total_of(lambda f, g: (g - own_theta * f) * (g - own_theta * f))
    at = lax.broadcasted_iota(jnp.int32, scal_x.shape[1:], 0)
    scal_x[x] = jnp.where(at == 0, square, jnp.where(at == 1, cross, rest))
    x_copies = [remote(scal_x.at[x], scal_x.at[x], device) for device in along_x]

    def hold_near2(side, part_of, group):
        for d in group:
            value = jnp.where(exist(side), near2[side, part_of, at_slot[d]], 0.0)
            hold(2 * side, rows_of(part_of, d), value)

    passed = []
    for (group, slots), copy in zip(groups, onward):
        for side in range(2):
            copy[side].wait_recv()
            passed.append((side, group, remote(near2.at[side, c, slots], near2.at[side, c, slots], mate)))
    for group, slots in groups:
        for side in range(2):
            hold_near2(side, c, group)
    for copy in x_copies:
        copy.wait_recv()
    scal_z[z] = scal_x[...]
    z_copies = [remote(scal_z.at[z], scal_z.at[z], device) for device in along_z]
    for side, group, copy in passed:
        copy.wait_recv()
        hold_near2(side, 1 - c, group)
    product(part2)
    second = scatter_sum(part2, sib2, sum2, box2)
    for copy in z_copies:
        copy.wait_recv()

    def all_of(i):
        return jnp.concatenate(
            [scal_z[a, b, i:i + 1, :] for a in range(n_z) for b in range(n_x)], axis=0
        )

    squares, crosses, rests = all_of(0), all_of(1), all_of(2)
    thetas = jnp.where(squares > 0, crosses / squares, 0.0)
    theta = jnp.sum(crosses, axis=0, keepdims=True) / jnp.sum(squares, axis=0, keepdims=True)
    gap = (thetas - theta) * jnp.sqrt(squares)
    energy = jnp.sum(rests + gap * gap, axis=0, keepdims=True)
    scale = lax.rsqrt(energy / (n_sec * block * block) + 1e-06)

    last[c, tile_rows(y, piece)] = scale * (second - theta * full[c, 0])
    mine = last.at[c, tile_rows(y, piece)]
    copies = {d: remote(mine, mine, along_y[d]) for d in FAR_FIRST}
    onward = [remote(mine, mine, mate)]
    for d in order[1:]:
        copies[n_y - d].wait_recv()
        here = last.at[c, tile_rows((y + d) % n_y, piece)]
        onward.append(remote(here, here, mate))
    for part_of in range(2):
        for d in order:
            where = rows_of(part_of, d)
            corr[where] = (full[part_of, at_slot[d]] - theta * field[where]) * scale
    image[tile_rows(c, half)] = last[c]
    for copy in onward:
        copy.wait_recv()
    image[tile_rows(1 - c, half)] = last[1 - c]
    for copy in sent:
        copy.wait_send()


def finish_kernel(corr, image, corr_out, image_out, sem):
    copies = [
        pltpu.make_async_copy(corr, corr_out.at[0], sem.at[0]),
        pltpu.make_async_copy(image, image_out.at[0], sem.at[1]),
    ]
    for copy in copies:
        copy.start()
    for copy in copies:
        copy.wait()


def local(n_sec, n_op, state, left, right, shift, rows, cols):
    terms, block = left.shape[0], state.shape[1]
    n_x = min(SEC_X, n_sec)
    n_y = n_op // 2
    half = block // 2
    piece = half // n_y
    f32, bf16 = jnp.float32, jnp.bfloat16
    n_copies = 84
    whole, halves = (block, block), (half, block)
    by_piece = (2, n_y, piece, block)
    in_hbm = [
        pltpu.with_memory_space_constraint(value, pltpu.HBM) for value in (state, left, right, shift)
    ]
    results = pl.pallas_call(
        functools.partial(kernel, (n_sec, n_op, terms, block)),
        out_shape=[pltpu.VMEM(whole, f32)] * 2,
        in_specs=[pl.BlockSpec(memory_space=pltpu.HBM)] * 4 + [pl.BlockSpec(memory_space=pl.ANY)] * 2,
        out_specs=[pl.BlockSpec(memory_space=pltpu.VMEM)] * 2,
        scratch_shapes=[
            pltpu.VMEM(whole, f32),
            pltpu.VMEM((terms,) + whole, f32),
            pltpu.VMEM((terms,) + whole, f32),
            pltpu.SMEM((terms,), jnp.int32),
            pltpu.SMEM((1,), jnp.int32),
            pltpu.SMEM((1,), jnp.int32),
            pltpu.VMEM((2, terms) + whole, bf16),
            pltpu.VMEM((2, terms) + whole, bf16),
            pltpu.VMEM((3, 2) + whole, bf16),
            pltpu.VMEM(whole, f32),
            pltpu.VMEM((2, 2) + halves, f32),
            pltpu.VMEM((2,) + by_piece, f32),
            pltpu.VMEM((2,) + halves, f32),
            pltpu.VMEM((2,) + halves, f32),
            pltpu.VMEM(halves, f32),
            pltpu.VMEM(halves, f32),
            pltpu.VMEM(halves, f32),
            pltpu.VMEM(halves, f32),
            pltpu.VMEM((n_y, piece, block), f32),
            pltpu.VMEM((n_y, piece, block), f32),
            pltpu.VMEM(by_piece, f32),
            pltpu.VMEM((2,) + halves, f32),
            pltpu.VMEM((8, block), jnp.int32),
            pltpu.VMEM((2, 8, block), jnp.int32),
            pltpu.VMEM((n_x, 8, block), f32),
            pltpu.VMEM((n_sec // n_x, n_x, 8, block), f32),
            pltpu.SemaphoreType.DMA((6,)),
            pltpu.SemaphoreType.DMA((n_copies,)),
            pltpu.SemaphoreType.DMA((n_copies,)),
        ],
        compiler_params=pltpu.CompilerParams(
            collective_id=0, has_side_effects=True, vmem_limit_bytes=40 << 20
        ),
        name="davidson",
    )(*in_hbm, rows, cols)
    return pl.pallas_call(
        finish_kernel,
        out_shape=[jax.ShapeDtypeStruct((1,) + whole, f32)] * 2,
        in_specs=[pl.BlockSpec(memory_space=pl.ANY)] * 2,
        out_specs=[pl.BlockSpec(memory_space=pltpu.HBM)] * 2,
        scratch_shapes=[pltpu.SemaphoreType.DMA((2,))],
        name="finish",
    )(*[pltpu.with_memory_space_constraint(value, pltpu.VMEM) for value in results])


def solution(mesh):
    in_specs = (
        P("sec", None, None),
        P("op", "sec", None, None),
        P("op", "sec", None, None),
        P("op"),
        P("sec"),
        P("sec"),
    )
    out_specs = (P("sec", None, None), P("sec", None, None))
    return jax.shard_map(
        functools.partial(local, mesh.shape["sec"], mesh.shape["op"]),
        mesh=mesh, in_specs=in_specs, out_specs=out_specs, check_vma=False,
    )
```

time: 68.6 us -> 60.5 us (0.88)
  local copies, waits for them, and re-layouts: 6.19 us -> 0 us
  Pallas kernels: 60.2 us -> 58.4 us
    unnamed x10 -> x0, local copies, waits for them, and re-layouts: 6.19 us -> none
    pallas_call x1, Pallas kernels: 60.2 us -> 57.6 us  [local(): pl.pallas_call(functools.partial(kernel, (n_sec, n_op, terms, block)), ou...]
    pallas_call x0 -> x1, Pallas kernels: none -> 0.81 us  [local(): pl.pallas_call(finish_kernel, out_shape=[jax.ShapeDtypeStruct((1,) + whol...]
where the time goes in v2:
time: 60.5 us; the launch traced here: 60.4 us
  Pallas kernels  58.4 us (97%)
  between operations  1.93 us (3%)
    pallas_call x1, Pallas kernels, local(): pl.pallas_call(functools.partial(kernel, (n_sec, n_op, terms, block)), ou...  57.6 us

profile of v2, /device:TPU:1, one launch (start us, length us, event | category | flops | bytes accessed | tf_op | source)
XLA Modules:
  0.0 60.4 jit_solution(10085207214884038057)
XLA Ops:
  1.9 57.6 %davidson.1 = (f32[256,256]{1,0:T(8,128)S(1)}, f32[256,256]{1,0:T(8,128)S(1)}) custom-call(f32[1,256,256]{2,1,0:T(8,128)} %state.1, f32[8,1,256,256]{3,2,1,0:T(8,128)} %left.1, f32[8,1,256,256]{3,2,1,0:T(8,128)} %right.1, s32[8]{0:T(128)} %shift.1, s32[1]{0:T(128)S(6)} %copy.8.rows, s32[1]{0:T(128)S(6)} %copy.9.cols), custom_call_target="tpu_custom_call" | custom-call | tf_op jit(solution)/shard_map/davidson/pallas_call | solution.py:295
  59.5 0.8 %finish.1 = (f32[1,256,256]{2,1,0:T(8,128)}, f32[1,256,256]{2,1,0:T(8,128)}) custom-call(f32[256,256]{1,0:T(8,128)S(1)} %get-tuple-element.4.corr, f32[256,256]{1,0:T(8,128)S(1)} %get-tuple-element.5.image), custom_call_target="tpu_custom_call" | custom-call | tf_op jit(solution)/shard_map/finish/pallas_call | solution.py:336

commit v3 on v2

v3 whole, which is shorter than its diff:
```python
import functools

import jax
import jax.numpy as jnp
from jax import lax
from jax.experimental import pallas as pl
from jax.experimental.pallas import tpu as pltpu
from jax.sharding import PartitionSpec as P

MESH = pl.DeviceIdType.MESH
SEC_X = 4
LANES = 128
HALO_CHUNKS = 2
FAR_FIRST = (4, 3, 5, 2, 6, 1, 7)
NEAR_FIRST = (1, 7, 2, 6, 3, 5, 4)
NN = (((1,), (0,)), ((), ()))
NT = (((1,), (1,)), ((), ()))


def split(value):
    high = value.astype(jnp.bfloat16)
    return high, (value - high.astype(jnp.float32)).astype(jnp.bfloat16)


def dot(a, b, dims):
    return lax.dot_general(a, b, dims, preferred_element_type=jnp.float32)


def dot3(a_high, a_low, b_high, b_low, dims):
    return dot(a_high, b_high, dims) + (dot(a_low, b_high, dims) + dot(a_high, b_low, dims))


def kernel(
    sizes,
    state, left, right, shift, rows, cols,
    corr, image,
    state_v, left_f, right_f, shift_s, rows_s, cols_s,
    left_c, right_c, vec_c,
    field, near1, near2, part1, part2, sib1, sib2, sum1, sum2, box1, box2,
    full, last, counts, near_counts, scal_x, scal_z,
    local_sem, send_sem, recv_sem, line_sem,
):
    n_sec, n_op, terms, block = sizes
    n_x = min(SEC_X, n_sec)
    n_z = n_sec // n_x
    n_y = n_op // 2
    half = block // 2
    piece = half // n_y
    s, o = lax.axis_index("sec"), lax.axis_index("op")
    y, c = lax.div(o, 2), lax.rem(o, 2)
    x, z = lax.rem(s, n_x), lax.div(s, n_x)
    mate = (s, y * 2 + (1 - c))
    after, before = (lax.rem(s + 1, n_sec), o), (lax.rem(s + n_sec - 1, n_sec), o)
    at_y = {0: y, **{d: lax.rem(y + d, n_y) for d in FAR_FIRST}}
    along_y = {d: (s, at_y[d] * 2 + c) for d in FAR_FIRST}
    along_x = [(z * n_x + lax.rem(x + d, n_x), o) for d in range(1, n_x)]
    along_z = [(lax.rem(z + d, n_z) * n_x + x, o) for d in range(1, n_z)]
    rows_of = {d: pl.ds(pl.multiple_of(at_y[d] * piece, piece), piece) for d in at_y}

    count = [0]
    sent = []

    def only(condition, action):
        if condition is None:
            action()
        else:
            pl.when(condition)(action)

    class Remote:
        def __init__(self, src, dst, device, to=None, came=None):
            i = count[0]
            count[0] += 1
            self.to, self.came = to, came
            self.copy = pltpu.make_async_remote_copy(
                src_ref=src, dst_ref=dst, send_sem=send_sem.at[i], recv_sem=recv_sem.at[i],
                device_id=device, device_id_type=MESH,
            )
            only(to, self.copy.start)
            sent.append(self)

        def wait_recv(self):
            only(self.came, self.copy.wait_recv)

        def wait_send(self):
            only(self.to, self.copy.wait_send)

    remote = Remote
    has_before, has_after = s > 0, s < n_sec - 1

    def to_after(src, near):
        return remote(src, near, after, has_after, has_before)

    def to_before(src, near):
        return remote(src, near, before, has_before, has_after)

    def tile_rows(index, size):
        return pl.ds(pl.multiple_of(index * size, size), size)

    def on_line(d):
        return ((z >= d, (s - d * n_x, o)), (z < n_z - d, (s + d * n_x, o)))

    def signal(semaphore, device):
        pl.semaphore_signal(semaphore, inc=1, device_id=device, device_id_type=MESH)

    def greet(semaphore, pairs):
        for condition, device in pairs:
            pl.when(condition)(functools.partial(signal, semaphore, device))

    def heard(pairs):
        return sum(condition.astype(jnp.int32) for condition, _ in pairs)

    always = [mate, *along_y.values(), *along_x]
    sometimes = [(has_after, after), (has_before, before), *on_line(1)]
    barrier = pltpu.get_barrier_semaphore()
    greet(barrier, sometimes)
    for device in always:
        signal(barrier, device)

    def load(i, src, dst):
        copy = pltpu.make_async_copy(src, dst, local_sem.at[i])
        copy.start()
        return copy

    small = [load(0, rows, rows_s), load(1, cols, cols_s), load(2, shift, shift_s)]
    pl.semaphore_wait(barrier, len(always) + heard(sometimes))
    greet(line_sem.at[0], on_line(1))

    chunk = half // HALO_CHUNKS
    chunks = [pl.ds(i * chunk, chunk) for i in range(HALO_CHUNKS)]
    halo = []
    for i, rows_at in enumerate(chunks):
        here = state.at[0, tile_rows(c * HALO_CHUNKS + i, chunk)]
        halo.append((
            to_after(here, near1.at[0, c, rows_at]), to_before(here, near1.at[1, c, rows_at])
        ))
    own_state = load(3, state.at[0], state_v)
    operators = [load(4, left.at[:, 0], left_f), load(5, right.at[:, 0], right_f)]
    for copy in small:
        copy.wait()
    n_rows, n_cols = rows_s[0], cols_s[0]
    at = lax.broadcasted_iota(jnp.int32, counts.shape, 0)
    counts[...] = jnp.where(at == 0, n_rows, n_cols)
    count_copies = [
        to_after(counts, near_counts.at[0]), to_before(counts, near_counts.at[1])
    ]

    def masked(value, row0, some_rows, some_cols):
        at_row = lax.broadcasted_iota(jnp.int32, value.shape, 0) + row0
        at_col = lax.broadcasted_iota(jnp.int32, value.shape, 1)
        return value * ((at_row < some_rows) & (at_col < some_cols)).astype(jnp.float32)

    def hold(slot, where, value):
        high, low = split(value)
        vec_c[slot, 0, where] = high
        vec_c[slot, 1, where] = low

    def product(part):
        total = None
        for k in range(terms):
            source = 1 - shift_s[k]
            inner = dot3(left_c[0, k], left_c[1, k], vec_c[source, 0], vec_c[source, 1], NN)
            high, low = split(inner)
            term = dot3(high, low, right_c[0, k], right_c[1, k], NT)
            total = term if total is None else total + term
        part[0] = total[:half]
        part[1] = total[half:]

    def product_sum(part, sib, summed, box):
        product(part)
        swap = remote(part.at[1 - c], sib, mate)
        swap.wait_recv()
        summed[...] = part[c] + sib[...]
        copies = {}
        for d in FAR_FIRST:
            copies[d] = remote(summed.at[rows_of[d]], box.at[d], along_y[d])
        total = summed[rows_of[0]]
        for d in NEAR_FIRST:
            copies[d].wait_recv()
            total = total + box[d]
        return masked(total, c * half + y * piece, n_rows, n_cols)

    exist = (has_before, has_after)
    for side in range(2):
        @pl.when(jnp.logical_not(exist[side]))
        def _():
            vec_c[2 * side] = jnp.zeros(vec_c.shape[1:], vec_c.dtype)

    own_state.wait()
    field[...] = masked(state_v[...], 0, n_rows, n_cols)
    hold(1, slice(None), field[...])
    for copy in operators:
        copy.wait()
    for k in range(terms):
        left_c[0, k], left_c[1, k] = split(left_f[k])
        right_c[0, k], right_c[1, k] = split(right_f[k])
    pl.semaphore_wait(line_sem.at[0], heard(on_line(1)))
    greet(line_sem.at[1], on_line(2))

    def pass_on(copy, side, here):
        copy.wait_recv()
        return remote(here, here, mate, exist[side], exist[side])

    passed = []
    for rows_at, both in zip(chunks, halo):
        for side in range(2):
            passed.append((side, pass_on(both[side], side, near1.at[side, c, rows_at])))

    def hold_near(side, part_of, i):
        value = masked(
            near1[side, part_of, chunks[i]], part_of * half + i * chunk,
            near_counts[side, 0:1, :], near_counts[side, 1:2, :],
        )
        hold(2 * side, tile_rows(part_of * HALO_CHUNKS + i, chunk), value)

    for side in range(2):
        count_copies[side].wait_recv()
        for i in range(HALO_CHUNKS):
            only(exist[side], functools.partial(hold_near, side, c, i))
    for i, (side, copy) in enumerate(passed):
        copy.wait_recv()
        only(exist[side], functools.partial(hold_near, side, 1 - c, i // 2))
    pl.semaphore_wait(line_sem.at[1], heard(on_line(2)))
    greet(line_sem.at[2], on_line(4))
    full[c, rows_of[0]] = product_sum(part1, sib1, sum1, box1)

    def gather(whole, send_on):
        mine = whole.at[c, rows_of[0]]
        copies = {d: remote(mine, mine, along_y[d]) for d in FAR_FIRST}
        send_on(rows_of[0])
        for d in NEAR_FIRST:
            copies[n_y - d].wait_recv()
            send_on(rows_of[d])

    to_mate, to_near = [], []

    def send_full(at):
        here = full.at[c, at]
        to_near.append((at, 0, to_after(here, near2.at[0, c, at])))
        to_near.append((at, 1, to_before(here, near2.at[1, c, at])))
        to_mate.append(remote(here, here, mate))

    gather(full, send_full)
    hold(1, tile_rows(c, half), full[c])
    for copy in to_mate:
        copy.wait_recv()
    hold(1, tile_rows(1 - c, half), full[1 - c])

    def total_of(term):
        value = term(field[:half], full[0]) + term(field[half:], full[1])
        return jnp.sum(jnp.sum(value, axis=0, keepdims=True), axis=1, keepdims=True)

    square = total_of(lambda f, g: f * f)
    cross = total_of(lambda f, g: f * g)
    own_theta = jnp.where(square > 0, cross / square, 0.0)
    rest = total_of(lambda f, g: (g - own_theta * f) * (g - own_theta * f))
    at = lax.broadcasted_iota(jnp.int32, scal_x.shape[1:], 0)
    scal_x[x] = jnp.where(at == 0, square, jnp.where(at == 1, cross, rest))
    x_copies = [remote(scal_x.at[x], scal_x.at[x], device) for device in along_x]

    def hold_near2(side, part_of):
        hold(2 * side, tile_rows(part_of, half), near2[side, part_of])

    passed = []
    for at, side, copy in to_near:
        passed.append(pass_on(copy, side, near2.at[side, c, at]))
    for side in range(2):
        only(exist[side], functools.partial(hold_near2, side, c))
    for copy in x_copies:
        copy.wait_recv()
    scal_z[z] = scal_x[...]
    pl.semaphore_wait(line_sem.at[2], heard(on_line(4)))
    z_copies = [remote(scal_z.at[z], scal_z.at[z], device) for device in along_z]
    for copy in passed:
        copy.wait_recv()
    for side in range(2):
        only(exist[side], functools.partial(hold_near2, side, 1 - c))
    last[c, rows_of[0]] = product_sum(part2, sib2, sum2, box2)
    to_mate = []

    def send_last(at):
        here = last.at[c, at]
        to_mate.append(remote(here, here, mate))

    gather(last, send_last)
    for copy in z_copies:
        copy.wait_recv()

    def all_of(i):
        return jnp.concatenate(
            [scal_z[a, b, i:i + 1, :] for a in range(n_z) for b in range(n_x)], axis=0
        )

    squares, crosses, rests = all_of(0), all_of(1), all_of(2)
    thetas = jnp.where(squares > 0, crosses / squares, 0.0)
    theta = jnp.sum(crosses, axis=0, keepdims=True) / jnp.sum(squares, axis=0, keepdims=True)
    gap = (thetas - theta) * jnp.sqrt(squares)
    energy = jnp.sum(rests + gap * gap, axis=0, keepdims=True)
    scale = lax.rsqrt(energy / (n_sec * block * block) + 1e-06)

    def finished(part_of):
        image[tile_rows(part_of, half)] = scale * (last[part_of] - theta * full[part_of])

    for part_of in range(2):
        where = slice(part_of * half, (part_of + 1) * half)
        corr[where] = (full[part_of] - theta * field[where]) * scale
    finished(c)
    for copy in to_mate:
        copy.wait_recv()
    finished(1 - c)
    for copy in sent:
        copy.wait_send()


def finish_kernel(corr, image, corr_out, image_out, sem):
    copies = [
        pltpu.make_async_copy(corr, corr_out.at[0], sem.at[0]),
        pltpu.make_async_copy(image, image_out.at[0], sem.at[1]),
    ]
    for copy in copies:
        copy.start()
    for copy in copies:
        copy.wait()


def local(n_sec, n_op, state, left, right, shift, rows, cols):
    terms, block = left.shape[0], state.shape[1]
    n_x = min(SEC_X, n_sec)
    n_y = n_op // 2
    half = block // 2
    piece = half // n_y
    f32, bf16 = jnp.float32, jnp.bfloat16
    n_copies = 128
    whole, halves = (block, block), (half, block)
    in_hbm = [
        pltpu.with_memory_space_constraint(value, pltpu.HBM) for value in (state, left, right, shift)
    ]
    results = pl.pallas_call(
        functools.partial(kernel, (n_sec, n_op, terms, block)),
        out_shape=[pltpu.VMEM(whole, f32)] * 2,
        in_specs=[pl.BlockSpec(memory_space=pltpu.HBM)] * 4 + [pl.BlockSpec(memory_space=pl.ANY)] * 2,
        out_specs=[pl.BlockSpec(memory_space=pltpu.VMEM)] * 2,
        scratch_shapes=[
            pltpu.VMEM(whole, f32),
            pltpu.VMEM((terms,) + whole, f32),
            pltpu.VMEM((terms,) + whole, f32),
            pltpu.SMEM((terms,), jnp.int32),
            pltpu.SMEM((1,), jnp.int32),
            pltpu.SMEM((1,), jnp.int32),
            pltpu.VMEM((2, terms) + whole, bf16),
            pltpu.VMEM((2, terms) + whole, bf16),
            pltpu.VMEM((3, 2) + whole, bf16),
            pltpu.VMEM(whole, f32),
            pltpu.VMEM((2, 2) + halves, f32),
            pltpu.VMEM((2, 2) + halves, f32),
            pltpu.VMEM((2,) + halves, f32),
            pltpu.VMEM((2,) + halves, f32),
            pltpu.VMEM(halves, f32),
            pltpu.VMEM(halves, f32),
            pltpu.VMEM(halves, f32),
            pltpu.VMEM(halves, f32),
            pltpu.VMEM((n_y, piece, block), f32),
            pltpu.VMEM((n_y, piece, block), f32),
            pltpu.VMEM((2,) + halves, f32),
            pltpu.VMEM((2,) + halves, f32),
            pltpu.VMEM((8, block), jnp.int32),
            pltpu.VMEM((2, 8, block), jnp.int32),
            pltpu.VMEM((n_x, 8, block), f32),
            pltpu.VMEM((n_sec // n_x, n_x, 8, block), f32),
            pltpu.SemaphoreType.DMA((6,)),
            pltpu.SemaphoreType.DMA((n_copies,)),
            pltpu.SemaphoreType.DMA((n_copies,)),
            pltpu.SemaphoreType.REGULAR((3,)),
        ],
        compiler_params=pltpu.CompilerParams(
            collective_id=0, has_side_effects=True, vmem_limit_bytes=40 << 20
        ),
        name="davidson",
    )(*in_hbm, rows, cols)
    return pl.pallas_call(
        finish_kernel,
        out_shape=[jax.ShapeDtypeStruct((1,) + whole, f32)] * 2,
        in_specs=[pl.BlockSpec(memory_space=pl.ANY)] * 2,
        out_specs=[pl.BlockSpec(memory_space=pltpu.HBM)] * 2,
        scratch_shapes=[pltpu.SemaphoreType.DMA((2,))],
        name="finish",
    )(*[pltpu.with_memory_space_constraint(value, pltpu.VMEM) for value in results])


def solution(mesh):
    in_specs = (
        P("sec", None, None),
        P("op", "sec", None, None),
        P("op", "sec", None, None),
        P("op"),
        P("sec"),
        P("sec"),
    )
    out_specs = (P("sec", None, None), P("sec", None, None))
    return jax.shard_map(
        functools.partial(local, mesh.shape["sec"], mesh.shape["op"]),
        mesh=mesh, in_specs=in_specs, out_specs=out_specs, check_vma=False,
    )
```

time: 60.5 us -> 55.1 us (0.911)
  Pallas kernels: 58.4 us -> 53 us
    pallas_call x1, Pallas kernels: 57.6 us -> 52.2 us  [local(): pl.pallas_call(functools.partial(kernel, (n_sec, n_op, terms, block)), ou...]
where the time goes in v3:
time: 55.1 us; the launch traced here: 55 us
  Pallas kernels  53 us (96%)
  between operations  1.93 us (4%)
    pallas_call x1, Pallas kernels, local(): pl.pallas_call(functools.partial(kernel, (n_sec, n_op, terms, block)), ou...  52.2 us

profile of v3, /device:TPU:1, one launch (start us, length us, event | category | flops | bytes accessed | tf_op | source)
XLA Modules:
  0.0 55.0 jit_solution(6166967737810996477)
XLA Ops:
  1.9 52.2 %davidson.1 = (f32[256,256]{1,0:T(8,128)S(1)}, f32[256,256]{1,0:T(8,128)S(1)}) custom-call(f32[1,256,256]{2,1,0:T(8,128)} %state.1, f32[8,1,256,256]{3,2,1,0:T(8,128)} %left.1, f32[8,1,256,256]{3,2,1,0:T(8,128)} %right.1, s32[8]{0:T(128)} %shift.1, s32[1]{0:T(128)S(6)} %copy.8.rows, s32[1]{0:T(128)S(6)} %copy.9.cols), custom_call_target="tpu_custom_call" | custom-call | tf_op jit(solution)/shard_map/davidson/pallas_call | solution.py:337
  54.2 0.8 %finish.1 = (f32[1,256,256]{2,1,0:T(8,128)}, f32[1,256,256]{2,1,0:T(8,128)}) custom-call(f32[256,256]{1,0:T(8,128)S(1)} %get-tuple-element.4.corr, f32[256,256]{1,0:T(8,128)S(1)} %get-tuple-element.5.image), custom_call_target="tpu_custom_call" | custom-call | tf_op jit(solution)/shard_map/finish/pallas_call | solution.py:379

commit v4 on v3

--- a/solution.py
+++ b/solution.py
@@ -165,9 +165,11 @@
         part[0] = total[:half]
         part[1] = total[half:]
 
-    def product_sum(part, sib, summed, box):
+    def product_sum(part, sib, summed, box, meanwhile=None):
         product(part)
         swap = remote(part.at[1 - c], sib, mate)
+        if meanwhile is not None:
+            meanwhile()
         swap.wait_recv()
         summed[...] = part[c] + sib[...]
         copies = {}
@@ -268,13 +270,17 @@
     for copy in x_copies:
         copy.wait_recv()
     scal_z[z] = scal_x[...]
-    pl.semaphore_wait(line_sem.at[2], heard(on_line(4)))
-    z_copies = [remote(scal_z.at[z], scal_z.at[z], device) for device in along_z]
+    z_copies = []
+
+    def send_scalars():
+        pl.semaphore_wait(line_sem.at[2], heard(on_line(4)))
+        z_copies.extend(remote(scal_z.at[z], scal_z.at[z], device) for device in along_z)
+
     for copy in passed:
         copy.wait_recv()
     for side in range(2):
         only(exist[side], functools.partial(hold_near2, side, 1 - c))
-    last[c, rows_of[0]] = product_sum(part2, sib2, sum2, box2)
+    last[c, rows_of[0]] = product_sum(part2, sib2, sum2, box2, send_scalars)
     to_mate = []
 
     def send_last(at):

time: 55.1 us -> 56.6 us (1.027)
  Pallas kernels: 53 us -> 54.6 us
    pallas_call x1, Pallas kernels: 52.2 us -> 53.7 us  [local(): pl.pallas_call(functools.partial(kernel, (n_sec, n_op, terms, block)), ou...]
where the time goes in v4:
time: 56.6 us; the launch traced here: 56.5 us
  Pallas kernels  54.6 us (96%)
  between operations  1.93 us (3%)
    pallas_call x1, Pallas kernels, local(): pl.pallas_call(functools.partial(kernel, (n_sec, n_op, terms, block)), ou...  53.7 us

profile of v4, /device:TPU:1, one launch (start us, length us, event | category | flops | bytes accessed | tf_op | source)
XLA Modules:
  0.0 56.5 jit_solution(8409288991416433487)
XLA Ops:
  1.9 53.7 %davidson.1 = (f32[256,256]{1,0:T(8,128)S(1)}, f32[256,256]{1,0:T(8,128)S(1)}) custom-call(f32[1,256,256]{2,1,0:T(8,128)} %state.1, f32[8,1,256,256]{3,2,1,0:T(8,128)} %left.1, f32[8,1,256,256]{3,2,1,0:T(8,128)} %right.1, s32[8]{0:T(128)} %shift.1, s32[1]{0:T(128)S(6)} %copy.8.rows, s32[1]{0:T(128)S(6)} %copy.9.cols), custom_call_target="tpu_custom_call" | custom-call | tf_op jit(solution)/shard_map/davidson/pallas_call | solution.py:343
  55.7 0.8 %finish.1 = (f32[1,256,256]{2,1,0:T(8,128)}, f32[1,256,256]{2,1,0:T(8,128)}) custom-call(f32[256,256]{1,0:T(8,128)S(1)} %get-tuple-element.4.corr, f32[256,256]{1,0:T(8,128)S(1)} %get-tuple-element.5.image), custom_call_target="tpu_custom_call" | custom-call | tf_op jit(solution)/shard_map/finish/pallas_call | solution.py:385
